TPU v7x, 32 devices: a whole 2x2x4 slice. The times are simulated.
32 devices in a mesh: seq: 4 (over x, core), chan: 8 (over z, y).
Axes of the slice: x: 2, y: 2, z: 4, core: 2. Of those that a mesh axis runs over, the one named last changes fastest.
Arguments:
- signal_in: bfloat16 [1024, 8192], P('seq', 'chan'), may hold values from -6 to 6
- gate_in: bfloat16 [1024, 8192], P('seq', 'chan'), may hold values from -6 to 6
- outer_gate: bfloat16 [1024, 8192], P('seq', 'chan'), may hold values from -6 to 6
- cotangent: bfloat16 [1024, 8192], P('seq', 'chan'), may hold values from -6 to 6
- residues: float32 [16, 512], replicated, may hold values from -4 to 4
- log_rates: float32 [16, 512], replicated, may hold values from -11 to -2.5
Outputs:
- grad_signal: bfloat16 [1024, 8192], P('seq', 'chan')
- grad_gate: bfloat16 [1024, 8192], P('seq', 'chan')
- grad_outer: bfloat16 [1024, 8192], P('seq', 'chan')
- grad_residues: float32 [16, 512], replicated
- grad_log_rates: float32 [16, 512], replicated
All inputs are finite; a program needn't handle non-finite values.
Results may differ from a plain program's by a relative error of at most 0.01.
Values may be sent and summed in bfloat16 or wider, within the bound.
A program may use at most 64 MiB of HBM per device.

v0:
```python
import functools
import math

import jax
import jax.numpy as jnp
from jax import lax
from jax.experimental import pallas as pl
from jax.experimental.pallas import tpu as pltpu
from jax.sharding import PartitionSpec as P

LANES = 128
SUB = 8
SEG = 16
f32 = jnp.float32
MESH = pl.DeviceIdType.MESH


def rows_of(ref, first, stride):
    return ref[pl.ds(first, SUB, stride=stride), :]


def spread(ref, row):
    return jnp.broadcast_to(ref[pl.ds(row, 1), :], (SUB, LANES))


def filter_lanes(block, cols, filters):
    start = lax.axis_index("chan") * cols + block * LANES
    return pl.ds(pl.multiple_of(lax.rem(start, filters), LANES), LANES)


def block_lanes(block):
    return pl.ds(pl.multiple_of(block * LANES, LANES), LANES)


def tree(values):
    while len(values) > 1:
        values = [values[i] + values[i + 1] for i in range(0, len(values), 2)]
    return values[0]


def state_block(scale, block, fl, sig, gate, outer, cot, res, logr, g_s, w_s, a_s, h_s, pw_s, st, lag_s, xs, ys, edge,
                moment, gsum):
    rows = sig.shape[0]
    modes = res.shape[0]
    segs = rows // SEG
    groups = segs // SUB
    g_s[...] = (sig[...].astype(f32) * gate[...].astype(f32)).astype(jnp.bfloat16).astype(f32)
    w_s[...] = (cot[...].astype(f32) * outer[...].astype(f32)).astype(jnp.bfloat16).astype(f32)
    rate = jnp.exp(logr[:, fl])
    amp = res[:, fl] * scale
    a = jnp.exp(-rate)
    a_s[...] = a
    power = jnp.ones((modes, LANES), f32)
    for u in range(SEG):
        pw_s[u * modes : (u + 1) * modes, :] = power
        h_s[u : u + 1, :] = jnp.sum(amp * power, 0, keepdims=True)
        power = power * a
    seg_decay = power

    @pl.loop(0, groups)
    def _(group):
        base = group * (SUB * SEG)
        for half in range(0, modes, SUB):
            decay = [spread(a_s, half + k) for k in range(SUB)]
            zero = jnp.zeros((SUB, LANES), f32)
            x, z, y, v = ([zero] * SUB for _ in range(4))
            for j in range(SEG):
                gj = rows_of(g_s, base + j, SEG)
                wj = rows_of(w_s, base + SEG - 1 - j, SEG)
                for k in range(SUB):
                    x[k] = decay[k] * (x[k] + gj)
                    z[k] = decay[k] * z[k] + x[k]
                    t = decay[k] * y[k]
                    y[k] = t + wj
                    v[k] = decay[k] * v[k] + t
            for k in range(SUB):
                at = pl.ds(pl.multiple_of((half + k) * segs + group * SUB, SUB), SUB)
                st[0, at, :] = x[k]
                st[1, at, :] = z[k]
                st[2, at, :] = y[k]
                st[3, at, :] = v[k]
        g = [rows_of(g_s, base + j, SEG) for j in range(SEG)]
        w = [rows_of(w_s, base + j, SEG) for j in range(SEG)]
        for u in range(SEG):
            total = w[u] * g[0]
            for j in range(u + 1, SEG):
                total = total + w[j] * g[j - u]
            lag_s[pl.ds(pl.multiple_of((group * SEG + u) * SUB, SUB), SUB), :] = total

    gr = jnp.zeros((modes, LANES), f32)
    gl = jnp.zeros((modes, LANES), f32)
    for u in range(SEG):
        total = lag_s[u * SUB : (u + 1) * SUB, :]
        for group in range(1, groups):
            first = (group * SEG + u) * SUB
            total = total + lag_s[first : first + SUB, :]
        term = jnp.sum(total, 0, keepdims=True) * pw_s[u * modes : (u + 1) * modes, :]
        gr = gr + term
        if u > 0:
            gl = gl + float(u) * term
    x = jnp.zeros((modes, LANES), f32)
    xd = x
    for seg in range(segs):
        at = pl.ds(seg, modes, stride=segs)
        e, d, y, v = (st[i, at, :] for i in range(4))
        xs[seg * modes : (seg + 1) * modes, :] = x
        if seg > 0:
            gr = gr + x * y
            gl = gl + (xd * y + x * v)
        xd = seg_decay * (xd + float(SEG) * x) + d
        x = seg_decay * x + e
    y = jnp.zeros((modes, LANES), f32)
    yv = y
    for seg in reversed(range(segs)):
        at = pl.ds(seg, modes, stride=segs)
        ys[seg * modes : (seg + 1) * modes, :] = y
        yv = st[3, at, :] + seg_decay * (yv + float(SEG) * y)
        y = st[2, at, :] + seg_decay * y
    edge[0, block] = x
    edge[1, block] = y
    moment[0] = xd
    moment[1] = yv
    gsum[0] = gr
    gsum[1] = gl


def inner_block(rows, g_s, w_s, h_s, conv, grad):
    @pl.loop(0, rows // (SEG * SUB))
    def _(group):
        base = group * (SUB * SEG)
        h = [spread(h_s, u) for u in range(SEG)]
        g = [rows_of(g_s, base + j, SEG) for j in range(SEG)]
        for j in range(SEG):
            forward = h[0] * g[j]
            for u in range(1, j + 1):
                forward = forward + h[u] * g[j - u]
            conv[pl.ds(base + j, SUB, stride=SEG), :] = forward
        w = [rows_of(w_s, base + j, SEG) for j in range(SEG)]
        for j in range(SEG):
            backward = h[0] * w[j]
            for u in range(1, SEG - j):
                backward = backward + h[u] * w[j + u]
            grad[pl.ds(base + j, SUB, stride=SEG), :] = backward


def gradient_block(scale, parts, span, block, fl, edges, edge, moment, gsum, res, logr, totals, carry):
    place = lax.axis_index("seq")
    rate = jnp.exp(logr[:, fl])
    x0 = jnp.zeros(rate.shape, f32)
    xm = x0
    y0 = x0
    for other in range(parts):
        ahead = jnp.maximum(place - 1 - other, 0).astype(f32) * float(span)
        behind = jnp.maximum(other - place - 1, 0).astype(f32) * float(span)
        value = edges[other, block]
        e = jnp.where(other < place, value, 0.0) * jnp.exp(-rate * ahead)
        x0 = x0 + e
        xm = xm + ahead * e
        y0 = y0 + jnp.where(other > place, value, 0.0) * jnp.exp(-rate * behind)
    carry[0] = x0
    carry[1] = y0
    w = edge[1, block]
    gr = gsum[0] + x0 * w
    gl = gsum[1] + x0 * moment[1] + xm * w + moment[0] * y0
    totals[0, :, fl] = totals[0, :, fl] + scale * gr
    totals[1, :, fl] = totals[1, :, fl] - scale * (res[:, fl] * rate) * gl


def output_block(scale, fl, res, logr, conv, grad, xs, ys, carry, a_s, p_s, q_s):
    rows = conv.shape[0]
    modes = res.shape[0]
    segs = rows // SEG
    rate = jnp.exp(logr[:, fl])
    amp = res[:, fl] * scale
    a_s[...] = jnp.exp(-rate)
    seg_decay = jnp.exp(-rate * float(SEG))
    p = amp * carry[0]
    q = amp * carry[1]
    for seg in range(segs):
        at = slice(seg * modes, (seg + 1) * modes)
        p_s[at, :] = amp * xs[at, :] + p
        p = p * seg_decay
        back = segs - 1 - seg
        at = slice(back * modes, (back + 1) * modes)
        q_s[at, :] = amp * ys[at, :] + q
        q = q * seg_decay

    @pl.loop(0, segs // SUB)
    def _(group):
        base = group * (SUB * SEG)
        for half in range(0, modes, SUB):
            decay = [spread(a_s, half + k) for k in range(SUB)]
            p = [rows_of(p_s, group * (SUB * modes) + half + k, modes) for k in range(SUB)]
            q = [rows_of(q_s, group * (SUB * modes) + half + k, modes) for k in range(SUB)]
            for j in range(SEG):
                at = pl.ds(base + j, SUB, stride=SEG)
                conv[at, :] = conv[at, :] + tree(p)
                q = [decay[k] * q[k] for k in range(SUB)]
                at = pl.ds(base + SEG - 1 - j, SUB, stride=SEG)
                grad[at, :] = grad[at, :] + tree(q)
                if j < SEG - 1:
                    p = [decay[k] * p[k] for k in range(SUB)]


def whole_kernel(
    scale, norm, parts, groups_chan,
    sig_h, gate_h, outer_h, cot_h, res_h, logr_h,
    out_sig_h, out_gate_h, out_outer_h, sums_h,
    ins, params, outs, g_s, w_s, conv, grad, xs, ys, edge, edges, moment, gsum, carry, h_s,
    a_s, pw_s, st, lag_s, p_s, q_s, totals, pieces, landed, slots, final,
    in_sem, param_sem, out_sem, edge_send, edge_recv, rs_send, rs_recv, mid_send, mid_recv, end_send, end_recv,
):
    rows, cols = sig_h.shape
    modes, filters = res_h.shape
    blocks = cols // LANES
    place = lax.axis_index("seq")
    column = lax.axis_index("chan")
    pairs = pair_size(groups_chan)
    barrier = pltpu.get_barrier_semaphore()

    def remote(src, dst, send, recv, device):
        return pltpu.make_async_remote_copy(
            src_ref=src, dst_ref=dst, send_sem=send, recv_sem=recv, device_id=device, device_id_type=MESH
        )

    low = lax.rem(column, pairs)
    high = column // pairs
    upper = groups_chan // pairs
    team = parts * pairs
    member = place * pairs + low

    def mate(index):
        return {"seq": index // pairs, "chan": high * pairs + lax.rem(index, pairs)}

    def tower(index):
        return {"chan": index * pairs + low}

    for d in range(1, team):
        pl.semaphore_signal(barrier, inc=1, device_id=mate(lax.rem(member + d, team)), device_id_type=MESH)
    for d in range(1, upper):
        pl.semaphore_signal(barrier, inc=1, device_id=tower(lax.rem(high + d, upper)), device_id_type=MESH)

    param_copies = [
        pltpu.make_async_copy(ref, params.at[i], param_sem.at[i]) for i, ref in enumerate((res_h, logr_h))
    ]
    for copy in param_copies:
        copy.start()

    def fetch(i, ref, block):
        return pltpu.make_async_copy(ref.at[:, block_lanes(block)], ins.at[i, block], in_sem.at[i, block])

    whole_inputs = (sig_h, gate_h, outer_h, cot_h)

    @pl.loop(0, blocks)
    def _(block):
        for i, ref in enumerate(whole_inputs):
            fetch(i, ref, block).start()

    for copy in param_copies:
        copy.wait()
    pl.semaphore_wait(barrier, team - 1 + upper - 1)
    res, logr = params.at[0], params.at[1]

    def edge_copy(d, block):
        other = lax.rem(place + d, parts)
        which = jnp.where(other > place, 0, 1)
        if block is None:
            src, dst = edge.at[which], edges.at[place]
        else:
            src, dst = edge.at[which, block], edges.at[place, block]
        return remote(src, dst, edge_send.at[d], edge_recv.at[d], {"seq": other})

    @pl.loop(0, blocks)
    def _(block):
        for i, ref in enumerate(whole_inputs):
            fetch(i, ref, block).wait()
        sig, gate, outer, cot = (ins.at[i, block] for i in range(4))
        state_block(
            scale, block, filter_lanes(block, cols, filters), sig, gate, outer, cot, res, logr,
            g_s.at[block], w_s.at[block], a_s, h_s.at[block], pw_s, st, lag_s, xs.at[block], ys.at[block], edge,
            moment.at[block], gsum.at[block],
        )
        for d in range(1, parts):
            edge_copy(d, block).start()

    def inner(first, last):
        @pl.loop(first, last)
        def _(block):
            inner_block(rows, g_s.at[block], w_s.at[block], h_s.at[block], conv.at[block], grad.at[block])

    early = (blocks + 1) // 2
    inner(0, early)
    for d in range(1, parts):
        source = lax.rem(place + parts - d, parts)
        remote(edge.at[0], edges.at[source], edge_send.at[d], edge_recv.at[d], {"seq": source}).wait_recv()
    totals[...] = jnp.zeros_like(totals)
    edges[place] = jnp.zeros_like(edge[0])

    @pl.loop(0, blocks)
    def _(block):
        gradient_block(
            scale, parts, rows, block, filter_lanes(block, cols, filters), edges, edge, moment.at[block],
            gsum.at[block], res, logr, totals, carry.at[block],
        )

    size = 2 * modes // team
    for p in range(team):
        which, first = divmod(p * size, modes)
        pieces[p] = totals[which, first : first + size, :]

    def scatter(d):
        other = lax.rem(member + d, team)
        return remote(pieces.at[other], landed.at[d], rs_send.at[d], rs_recv.at[d], mate(other))

    def middle(d, back=False):
        other = lax.rem(high + (upper - d if back else d), upper)
        slot = slots.at[other if back else high]
        return remote(slot, slot, mid_send.at[d], mid_recv.at[d], tower(other))

    def ending(d, back=False):
        other = lax.rem(member + (team - d if back else d), team)
        slot = final.at[other if back else member]
        return remote(slot, slot, end_send.at[d], end_recv.at[d], mate(other))

    for d in range(1, team):
        scatter(d).start()
    inner(early, blocks)

    def put(i, block):
        target = (out_sig_h, out_gate_h, out_outer_h)[i]
        return pltpu.make_async_copy(outs.at[i, block], target.at[:, block_lanes(block)], out_sem.at[i, block])

    def outputs(first, last):
        if first == last:
            return

        @pl.loop(first, last)
        def _(block):
            output_block(
                scale, filter_lanes(block, cols, filters), res, logr, conv.at[block], grad.at[block], xs.at[block],
                ys.at[block], carry.at[block], a_s, p_s, q_s,
            )
            d = grad[block]
            outs[0, block] = (d * ins[1, block].astype(f32)).astype(jnp.bfloat16)
            outs[1, block] = (d * ins[0, block].astype(f32)).astype(jnp.bfloat16)
            outs[2, block] = (conv[block] * ins[3, block].astype(f32)).astype(jnp.bfloat16)
            for i in range(3):
                put(i, block).start()

    first_stop = blocks // 8
    second_stop = blocks - blocks // 4
    outputs(0, first_stop)
    for d in range(1, team):
        scatter(d).wait_recv()
    mine = pieces[member]
    for d in range(1, team):
        mine = mine + landed[d]
    slots[high] = mine
    for d in range(1, upper):
        middle(d).start()
    outputs(first_stop, second_stop)
    for d in range(1, upper):
        middle(d, back=True).wait_recv()
    summed = slots[0]
    for other in range(1, upper):
        summed = summed + slots[other]
    final[member] = norm * summed
    for d in range(1, team):
        ending(d).start()
    outputs(second_stop, blocks)
    for d in range(1, team):
        ending(d, back=True).wait_recv()
    for p in range(team):
        which, first = divmod(p * size, modes)
        sums_h[which, first : first + size, :] = final[p]

    for d in range(1, parts):
        edge_copy(d, None).wait_send()
    for d in range(1, team):
        scatter(d).wait_send()
        ending(d).wait_send()
    for d in range(1, upper):
        middle(d).wait_send()

    @pl.loop(0, blocks)
    def _(block):
        for i in range(3):
            put(i, block).wait()


def pass_kernel(sig, gate, outer, sums, out_sig, out_gate, out_outer, out_res, out_rate, held, sums_held, sem_in, sem_out):
    chunks, depth = held.shape[1:3]
    todo = []
    for i, (src, dst) in enumerate(((sig, out_sig), (gate, out_gate), (outer, out_outer))):
        for c in range(chunks):
            at = pl.ds(c * depth, depth)
            todo.append((src.at[at, :], held.at[i, c], dst.at[at, :]))
    for i, dst in enumerate((out_res, out_rate)):
        todo.append((sums.at[i], sums_held.at[i], dst))
    into = [pltpu.make_async_copy(src, mid, sem_in.at[n]) for n, (src, mid, _) in enumerate(todo)]
    out = [pltpu.make_async_copy(mid, dst, sem_out.at[n]) for n, (_, mid, dst) in enumerate(todo)]
    for copy in into:
        copy.start()
    for first, second in zip(into, out):
        first.wait()
        second.start()
    for copy in out:
        copy.wait()


def pair_size(columns):
    return 2 if columns % 2 == 0 else 1


def on_device(signal_in, gate_in, outer_gate, cotangent, residues, log_rates):
    parts = lax.axis_size("seq")
    groups_chan = lax.axis_size("chan")
    rows, cols = signal_in.shape
    modes, filters = residues.shape
    total = parts * rows
    blocks = cols // LANES
    segs = rows // SEG
    groups = segs // SUB
    pairs = pair_size(groups_chan)
    team = parts * pairs
    upper = groups_chan // pairs
    size = 2 * modes // team
    scale = float(total) ** (-0.5)
    norm = float(total * cols * groups_chan // filters) ** (-0.5)
    whole = pl.BlockSpec(memory_space=pltpu.VMEM)
    far = pl.BlockSpec(memory_space=pl.ANY)
    shape = jax.ShapeDtypeStruct
    small = pltpu.VMEM((modes, LANES), f32)
    tiles = pltpu.VMEM((blocks, rows, LANES), f32)
    states = pltpu.VMEM((blocks, segs * modes, LANES), f32)
    pair = pltpu.VMEM((blocks, 2, modes, LANES), f32)
    dma = pltpu.SemaphoreType.DMA
    narrow = shape((rows, cols), jnp.bfloat16)
    *products, sums = pl.pallas_call(
        functools.partial(whole_kernel, scale, norm, parts, groups_chan),
        out_shape=(
            narrow,
            narrow,
            narrow,
            shape((2, modes, filters), f32),
        ),
        in_specs=[pl.BlockSpec(memory_space=pltpu.HBM)] * 6,
        out_specs=(far, far, far, whole),
        scratch_shapes=[
            pltpu.VMEM((4, blocks, rows, LANES), jnp.bfloat16),
            pltpu.VMEM((2, modes, filters), f32),
            pltpu.VMEM((3, blocks, rows, LANES), jnp.bfloat16),
            tiles,
            tiles,
            tiles,
            tiles,
            states,
            states,
            pltpu.VMEM((2, blocks, modes, LANES), f32),
            pltpu.VMEM((parts, blocks, modes, LANES), f32),
            pair,
            pair,
            pair,
            pltpu.VMEM((blocks, SEG, LANES), f32),
            small,
            pltpu.VMEM((SEG * modes, LANES), f32),
            pltpu.VMEM((4, modes * segs, LANES), f32),
            pltpu.VMEM((groups * SEG * SUB, LANES), f32),
            pltpu.VMEM((segs * modes, LANES), f32),
            pltpu.VMEM((segs * modes, LANES), f32),
            pltpu.VMEM((2, modes, filters), f32),
            pltpu.VMEM((team, size, filters), f32),
            pltpu.VMEM((team, size, filters), f32),
            pltpu.VMEM((upper, size, filters), f32),
            pltpu.VMEM((team, size, filters), f32),
            dma((4, blocks)),
            dma((2,)),
            dma((3, blocks)),
            dma((parts,)),
            dma((parts,)),
            dma((team,)),
            dma((team,)),
            dma((upper,)),
            dma((upper,)),
            dma((team,)),
            dma((team,)),
        ],
        compiler_params=pltpu.CompilerParams(
            collective_id=0, has_side_effects=True
        ),
        name="whole",
    )(signal_in, gate_in, outer_gate, cotangent, residues, log_rates)
    chunks = 2
    return pl.pallas_call(
        pass_kernel,
        out_shape=(narrow, narrow, narrow, shape((modes, filters), f32), shape((modes, filters), f32)),
        in_specs=[far] * 4,
        out_specs=(far,) * 5,
        scratch_shapes=[
            pltpu.VMEM((3, chunks, rows // chunks, cols), jnp.bfloat16),
            pltpu.VMEM((2, modes, filters), f32),
            dma((3 * chunks + 2,)),
            dma((3 * chunks + 2,)),
        ],
        name="passed",
    )(*products, sums)


def solution(mesh):
    placed = (P("seq", "chan"), P("seq", "chan"), P("seq", "chan"), P("seq", "chan"), P(), P())
    return jax.shard_map(
        on_device,
        mesh=mesh,
        in_specs=placed,
        out_specs=(P("seq", "chan"), P("seq", "chan"), P("seq", "chan"), P(), P()),
        check_vma=False,
    )
```

profile of v0, /device:TPU:0, one launch (start us, length us, event | category | flops | bytes accessed | tf_op | source)
XLA Modules:
  0.0 32.0 jit_solution(2389705340510823806)
XLA Ops:
  0.6 29.1 %whole.1 = (bf16[256,1024]{1,0:T(8,128)(2,1)}, bf16[256,1024]{1,0:T(8,128)(2,1)}, bf16[256,1024]{1,0:T(8,128)(2,1)}, f32[2,16,512]{2,1,0:T(8,128)}) custom-call(bf16[256,1024]{1,0:T(8,128)(2,1)} %sig_h.1, bf16[256,1024]{1,0:T(8,128)(2,1)} %gate_h.1, bf16[256,1024]{1,0:T(8,128)(2,1)} %outer_h.1, bf16[256,1024]{1,0:T(8,128)(2,1)} %cot_h.1, f32[16,512]{1,0:T(8,128)} %res_h.1, ...), custom_call_target="tpu_custom_call" | custom-call | tf_op jit(solution)/shard_map/whole/pallas_call | solution.py:439
  29.8 2.2 %passed.1 = (bf16[256,1024]{1,0:T(8,128)(2,1)}, bf16[256,1024]{1,0:T(8,128)(2,1)}, bf16[256,1024]{1,0:T(8,128)(2,1)}, f32[16,512]{1,0:T(8,128)}, f32[16,512]{1,0:T(8,128)}) custom-call(bf16[256,1024]{1,0:T(8,128)(2,1)} %get-tuple-element.9.sig, bf16[256,1024]{1,0:T(8,128)(2,1)} %get-tuple-element.10.gate, bf16[256,1024]{1,0:T(8,128)(2,1)} %get-tuple-element.11.outer, ...), custom_call_target="tpu_custom_call" | custom-call | tf_op jit(solution)/shard_map/passed/pallas_call | solution.py:494
where the time goes:
time: 32.2 us; the launch traced here: 32 us
  Pallas kernels  31.4 us (98%)
  between operations  0.64 us (2%)
    pallas_call x1, Pallas kernels, on_device(): pl.pallas_call(functools.partial(whole_kernel, scale, norm, parts, groups...  29.1 us
    pallas_call x1, Pallas kernels, on_device(): pl.pallas_call(pass_kernel, out_shape=(narrow, narrow, narrow, shape((mod...  2.23 us

commit v1 on v0

--- a/solution.py
+++ b/solution.py
@@ -341,11 +341,10 @@
                 ys.at[block], carry.at[block], a_s, p_s, q_s,
             )
             d = grad[block]
-            outs[0, block] = (d * ins[1, block].astype(f32)).astype(jnp.bfloat16)
-            outs[1, block] = (d * ins[0, block].astype(f32)).astype(jnp.bfloat16)
-            outs[2, block] = (conv[block] * ins[3, block].astype(f32)).astype(jnp.bfloat16)
-            for i in range(3):
-                put(i, block).start()
+            at = block_lanes(block)
+            out_sig_h[:, at] = (d * ins[1, block].astype(f32)).astype(jnp.bfloat16)
+            out_gate_h[:, at] = (d * ins[0, block].astype(f32)).astype(jnp.bfloat16)
+            out_outer_h[:, at] = (conv[block] * ins[3, block].astype(f32)).astype(jnp.bfloat16)
 
     first_stop = blocks // 8
     second_stop = blocks - blocks // 4
@@ -382,29 +381,13 @@
     for d in range(1, upper):
         middle(d).wait_send()
 
-    @pl.loop(0, blocks)
-    def _(block):
-        for i in range(3):
-            put(i, block).wait()
-
-
-def pass_kernel(sig, gate, outer, sums, out_sig, out_gate, out_outer, out_res, out_rate, held, sums_held, sem_in, sem_out):
-    chunks, depth = held.shape[1:3]
-    todo = []
-    for i, (src, dst) in enumerate(((sig, out_sig), (gate, out_gate), (outer, out_outer))):
-        for c in range(chunks):
-            at = pl.ds(c * depth, depth)
-            todo.append((src.at[at, :], held.at[i, c], dst.at[at, :]))
-    for i, dst in enumerate((out_res, out_rate)):
-        todo.append((sums.at[i], sums_held.at[i], dst))
-    into = [pltpu.make_async_copy(src, mid, sem_in.at[n]) for n, (src, mid, _) in enumerate(todo)]
-    out = [pltpu.make_async_copy(mid, dst, sem_out.at[n]) for n, (_, mid, dst) in enumerate(todo)]
-    for copy in into:
+
+def pass_kernel(sig, gate, outer, sums, out_sig, out_gate, out_outer, out_res, out_rate, sem):
+    pairs = ((sig, out_sig), (gate, out_gate), (outer, out_outer), (sums.at[0], out_res), (sums.at[1], out_rate))
+    copies = [pltpu.make_async_copy(src, dst, sem.at[n]) for n, (src, dst) in enumerate(pairs)]
+    for copy in copies:
         copy.start()
-    for first, second in zip(into, out):
-        first.wait()
-        second.start()
-    for copy in out:
+    for copy in copies:
         copy.wait()
 
 
@@ -439,13 +422,13 @@
     *products, sums = pl.pallas_call(
         functools.partial(whole_kernel, scale, norm, parts, groups_chan),
         out_shape=(
-            narrow,
-            narrow,
-            narrow,
-            shape((2, modes, filters), f32),
+            pltpu.VMEM((rows, cols), jnp.bfloat16),
+            pltpu.VMEM((rows, cols), jnp.bfloat16),
+            pltpu.VMEM((rows, cols), jnp.bfloat16),
+            pltpu.VMEM((2, modes, filters), f32),
         ),
         in_specs=[pl.BlockSpec(memory_space=pltpu.HBM)] * 6,
-        out_specs=(far, far, far, whole),
+        out_specs=(whole,) * 4,
         scratch_shapes=[
             pltpu.VMEM((4, blocks, rows, LANES), jnp.bfloat16),
             pltpu.VMEM((2, modes, filters), f32),
@@ -490,20 +473,14 @@
         ),
         name="whole",
     )(signal_in, gate_in, outer_gate, cotangent, residues, log_rates)
-    chunks = 2
     return pl.pallas_call(
         pass_kernel,
         out_shape=(narrow, narrow, narrow, shape((modes, filters), f32), shape((modes, filters), f32)),
-        in_specs=[far] * 4,
+        in_specs=[whole] * 4,
         out_specs=(far,) * 5,
-        scratch_shapes=[
-            pltpu.VMEM((3, chunks, rows // chunks, cols), jnp.bfloat16),
-            pltpu.VMEM((2, modes, filters), f32),
-            dma((3 * chunks + 2,)),
-            dma((3 * chunks + 2,)),
-        ],
+        scratch_shapes=[dma((5,))],
         name="passed",
-    )(*products, sums)
+    )(*(pltpu.with_memory_space_constraint(a, pltpu.VMEM) for a in (*products, sums)))
 
 
 def solution(mesh):

time: 32.2 us -> 30.4 us (0.944)
  Pallas kernels: 31.4 us -> 29.6 us
    pallas_call x1, Pallas kernels: 2.23 us -> 1.19 us  [on_device(): pl.pallas_call(pass_kernel, out_shape=(narrow, narrow, narrow, shape((mod...]
    pallas_call x1, Pallas kernels: 29.1 us -> 28.4 us  [on_device(): pl.pallas_call(functools.partial(whole_kernel, scale, norm, parts, groups...]
where the time goes in v1:
time: 30.4 us; the launch traced here: 30.3 us
  Pallas kernels  29.6 us (97%)
  between operations  0.64 us (2%)
    pallas_call x1, Pallas kernels, on_device(): pl.pallas_call(functools.partial(whole_kernel, scale, norm, parts, groups...  28.4 us
    pallas_call x1, Pallas kernels, on_device(): pl.pallas_call(pass_kernel, out_shape=(narrow, narrow, narrow, shape((mod...  1.19 us

profile of v1, /device:TPU:0, one launch (start us, length us, event | category | flops | bytes accessed | tf_op | source)
XLA Modules:
  0.0 30.3 jit_solution(15320912674768754415)
XLA Ops:
  0.6 28.4 %whole.1 = (bf16[256,1024]{1,0:T(8,128)(2,1)S(1)}, bf16[256,1024]{1,0:T(8,128)(2,1)S(1)}, bf16[256,1024]{1,0:T(8,128)(2,1)S(1)}, f32[2,16,512]{2,1,0:T(8,128)S(1)}) custom-call(bf16[256,1024]{1,0:T(8,128)(2,1)} %sig_h.1, bf16[256,1024]{1,0:T(8,128)(2,1)} %gate_h.1, bf16[256,1024]{1,0:T(8,128)(2,1)} %outer_h.1, bf16[256,1024]{1,0:T(8,128)(2,1)} %cot_h.1, ...), custom_call_target="tpu_custom_call" | custom-call | tf_op jit(solution)/shard_map/whole/pallas_call | solution.py:422
  29.1 1.2 %passed.1 = (bf16[256,1024]{1,0:T(8,128)(2,1)}, bf16[256,1024]{1,0:T(8,128)(2,1)}, bf16[256,1024]{1,0:T(8,128)(2,1)}, f32[16,512]{1,0:T(8,128)}, f32[16,512]{1,0:T(8,128)}) custom-call(bf16[256,1024]{1,0:T(8,128)(2,1)S(1)} %get-tuple-element.9.sig, bf16[256,1024]{1,0:T(8,128)(2,1)S(1)} %get-tuple-element.10.gate, ...), custom_call_target="tpu_custom_call" | custom-call | tf_op jit(solution)/shard_map/passed/pallas_call | solution.py:476

commit v2 on v1

v2 whole, which is shorter than its diff:
```python
import functools
import math

import jax
import jax.numpy as jnp
from jax import lax
from jax.experimental import pallas as pl
from jax.experimental.pallas import tpu as pltpu
from jax.sharding import PartitionSpec as P

LANES = 128
SUB = 8
SEG = 16
PACK = 16
f32 = jnp.float32
bf16 = jnp.bfloat16
MESH = pl.DeviceIdType.MESH


def rows_of(ref, first, stride):
    return ref[pl.ds(first, SUB, stride=stride), :]


def spread(ref, row):
    return jnp.broadcast_to(ref[pl.ds(row, 1), :], (SUB, LANES))


def spread_narrow(ref, row):
    return jnp.broadcast_to(ref[pl.ds(row, 1), :], (PACK, LANES)).astype(bf16)


def block_lanes(block):
    return pl.ds(pl.multiple_of(block * LANES, LANES), LANES)


def filter_lanes(block, cols, filters):
    start = lax.axis_index("chan") * cols + block * LANES
    return pl.ds(pl.multiple_of(lax.rem(start, filters), LANES), LANES)


def tree(values):
    while len(values) > 1:
        paired = [values[i] + values[i + 1] for i in range(0, len(values) - 1, 2)]
        values = paired + values[len(paired) * 2 :]
    return values[0]


def moments(terms, last):
    quads, weighted = [], []
    for first in range(0, len(terms), 4):
        p = [terms[first]]
        for term in terms[first + 1 : first + 4]:
            p.append(p[-1] + term)
        quads.append(p[3])
        weighted.append(tree(p if last else p[:3]))
    q = [quads[0]]
    for quad in quads[1:]:
        q.append(q[-1] + quad)
    return q[-1], tree(weighted) + 4.0 * tree(q[:-1])


def state_block(scale, place, fb, local, fl, ins, res, logr, g_s, w_s, gt, wt, h_s, pw_s, st, lag_s, xs, ys, edges):
    rows = g_s.shape[1]
    modes = res.shape[0]
    segs = rows // SEG
    reps = g_s.shape[0] // local
    rate = jnp.exp(logr[:, fl])
    amp = res[:, fl] * scale
    a = jnp.exp(-rate)
    power = jnp.ones((modes, LANES), f32)
    for u in range(SEG + 1):
        pw_s[u * modes : (u + 1) * modes, :] = power
        if u < SEG:
            h_s[fb, u : u + 1, :] = jnp.sum(amp * power, 0, keepdims=True)
            power = power * a
    seg_decay = power

    for rep in range(reps):
        block = rep * local + fb
        sig, gate, outer, cot = (ins[i, block].astype(f32) for i in range(4))
        g_s[block] = (sig * gate).astype(bf16).astype(f32)
        w_s[block] = (cot * outer).astype(bf16).astype(f32)
        for src, dst in ((g_s.at[block], gt), (w_s.at[block], wt)):
            for part in range(segs // PACK):
                base = part * PACK * SEG
                for j in range(SEG):
                    halves = [rows_of(src, base + half * SUB * SEG + j, SEG) for half in range(PACK // SUB)]
                    dst[rep, part, j * PACK : (j + 1) * PACK, :] = jnp.concatenate(halves, 0).astype(bf16)

    def phase(ref, rep, part, j):
        return ref[rep, part, j * PACK : (j + 1) * PACK, :]

    for k in range(modes):
        powers = [spread_narrow(pw_s, e * modes + k) for e in range(SEG + 1)]
        for rep in range(reps):
            for part in range(segs // PACK):
                x, d = moments([powers[SEG - j] * phase(gt, rep, part, j) for j in range(SEG)], True)
                back = [powers[j] * phase(wt, rep, part, j) for j in range(SEG - 1, 0, -1)]
                y, v = moments(back + [phase(wt, rep, part, 0)], False)
                at = slice(k * segs + part * PACK, k * segs + (part + 1) * PACK)
                for i, value in enumerate((x, d, y, v)):
                    st[rep, i, at, :] = value.astype(f32)

    lags = [None] * SEG
    for rep in range(reps):
        for part in range(segs // PACK):
            g = [phase(gt, rep, part, j) for j in range(SEG)]
            w = [phase(wt, rep, part, j) for j in range(SEG)]
            for u in range(SEG):
                total = tree([w[j] * g[j - u] for j in range(u, SEG)]).astype(f32)
                total = total[:SUB] + total[SUB:]
                if rep + part == 0:
                    lag_s[u * SUB : (u + 1) * SUB, :] = total
                else:
                    lag_s[u * SUB : (u + 1) * SUB, :] += total

    gr = jnp.zeros((modes, LANES), f32)
    gl = jnp.zeros((modes, LANES), f32)
    for u in range(SEG):
        total = jnp.sum(lag_s[u * SUB : (u + 1) * SUB, :], 0, keepdims=True)
        term = total * pw_s[u * modes : (u + 1) * modes, :]
        gr = gr + term
        if u > 0:
            gl = gl + float(u) * term
    zero = jnp.zeros((modes, LANES), f32)
    for rep in range(reps):
        block = rep * local + fb
        x, xd = zero, zero
        for seg in range(segs):
            at = pl.ds(seg, modes, stride=segs)
            e, d, y, v = (st[rep, i, at, :] for i in range(4))
            xs[block, seg * modes : (seg + 1) * modes, :] = x
            if seg > 0:
                gr = gr + x * y
                gl = gl + (xd * y + x * v)
            xd = seg_decay * (xd + float(SEG) * x) + d
            x = seg_decay * x + e
        y, yv = zero, zero
        for seg in reversed(range(segs)):
            at = pl.ds(seg, modes, stride=segs)
            ys[block, seg * modes : (seg + 1) * modes, :] = y
            yv = st[rep, 3, at, :] + seg_decay * (yv + float(SEG) * y)
            y = st[rep, 2, at, :] + seg_decay * y
        for i, value in enumerate((x, y, xd, yv)):
            edges[place, fb, i * reps + rep] = value.astype(bf16)
    edges[place, fb, 4 * reps] = gr.astype(bf16)
    edges[place, fb, 4 * reps + 1] = gl.astype(bf16)


def inner_block(rows, g_s, w_s, h_s, conv, grad):
    @pl.loop(0, rows // (SEG * SUB))
    def _(group):
        base = group * (SUB * SEG)
        h = [spread(h_s, u) for u in range(SEG)]
        g = [rows_of(g_s, base + j, SEG) for j in range(SEG)]
        for j in range(SEG):
            forward = h[0] * g[j]
            for u in range(1, j + 1):
                forward = forward + h[u] * g[j - u]
            conv[pl.ds(base + j, SUB, stride=SEG), :] = forward
        w = [rows_of(w_s, base + j, SEG) for j in range(SEG)]
        for j in range(SEG):
            backward = h[0] * w[j]
            for u in range(1, SEG - j):
                backward = backward + h[u] * w[j + u]
            grad[pl.ds(base + j, SUB, stride=SEG), :] = backward


def gradient_block(scale, span, fb, fl, edges, res, logr):
    parts = edges.shape[0]
    reps = edges.shape[2] // 4
    rate = jnp.exp(logr[:, fl])
    decay = jnp.exp(-rate * float(span))

    def value(source, i):
        return edges[source, fb, i].astype(f32)

    gr = tree([value(source, 4 * reps) for source in range(parts)])
    gl = tree([value(source, 4 * reps + 1) for source in range(parts)])
    for rep in range(reps):
        x = value(0, rep)
        xd = value(0, 2 * reps + rep)
        for source in range(1, parts):
            y = value(source, reps + rep)
            gr = gr + x * y
            gl = gl + (x * value(source, 3 * reps + rep) + xd * y)
            if source < parts - 1:
                xd = (xd + float(span) * x) * decay + value(source, 2 * reps + rep)
                x = x * decay + value(source, rep)
    return scale * gr, -scale * (res[:, fl] * rate) * gl


def carry_block(span, fb, rep, fl, edges, logr, carry):
    place = lax.axis_index("seq")
    parts = edges.shape[0]
    reps = edges.shape[2] // 4
    decay = jnp.exp(-jnp.exp(logr[:, fl]) * float(span))
    values = []
    for source in range(parts):
        which = jnp.where(source > place, reps, 0)
        values.append(edges[source, fb, which + rep].astype(f32))
    x = jnp.zeros(decay.shape, f32)
    y = x
    for source in range(parts):
        x = jnp.where(source < place, x * decay + values[source], x)
        back = parts - 1 - source
        y = jnp.where(back > place, y * decay + values[back], y)
    carry[0] = x
    carry[1] = y


def output_block(scale, fl, res, logr, conv, grad, xs, ys, carry, a_s, p_s, q_s):
    rows = conv.shape[0]
    modes = res.shape[0]
    segs = rows // SEG
    rate = jnp.exp(logr[:, fl])
    amp = res[:, fl] * scale
    a_s[...] = jnp.exp(-rate)
    seg_decay = jnp.exp(-rate * float(SEG))
    p = amp * carry[0]
    q = amp * carry[1]
    for seg in range(segs):
        at = slice(seg * modes, (seg + 1) * modes)
        p_s[at, :] = amp * xs[at, :] + p
        p = p * seg_decay
        back = segs - 1 - seg
        at = slice(back * modes, (back + 1) * modes)
        q_s[at, :] = amp * ys[at, :] + q
        q = q * seg_decay

    @pl.loop(0, segs // SUB)
    def _(group):
        base = group * (SUB * SEG)
        for half in range(0, modes, SUB):
            decay = [spread(a_s, half + k) for k in range(SUB)]
            p = [rows_of(p_s, group * (SUB * modes) + half + k, modes) for k in range(SUB)]
            q = [rows_of(q_s, group * (SUB * modes) + half + k, modes) for k in range(SUB)]
            for j in range(SEG):
                at = pl.ds(base + j, SUB, stride=SEG)
                conv[at, :] = conv[at, :] + tree(p)
                q = [decay[k] * q[k] for k in range(SUB)]
                at = pl.ds(base + SEG - 1 - j, SUB, stride=SEG)
                grad[at, :] = grad[at, :] + tree(q)
                if j < SEG - 1:
                    p = [decay[k] * p[k] for k in range(SUB)]


def whole_kernel(
    scale, norm, parts, groups_chan, owners,
    sig_h, gate_h, outer_h, cot_h, res_h, logr_h,
    out_sig, out_gate, out_outer, sums,
    ins, params, g_s, w_s, conv, grad, xs, ys, edges, carry, h_s, gt, wt,
    a_s, pw_s, st, lag_s, p_s, q_s, slots, final,
    in_sem, param_sem, edge_send, edge_recv, mid_send, mid_recv, end_send, end_recv,
):
    rows, cols = sig_h.shape
    modes, filters = res_h.shape
    blocks = cols // LANES
    local = edges.shape[1]
    reps = blocks // local
    per = local // owners
    kinds = final.shape[1]
    place = lax.axis_index("seq")
    column = lax.axis_index("chan")
    own = lax.rem(place, owners)
    cell = place - own
    barrier = pltpu.get_barrier_semaphore()

    def each(first, last, fn):
        if last - first <= 8:
            for d in range(first, last):
                fn(d)
        else:
            pl.loop(first, last)(fn)

    def remote(src, dst, send, recv, device):
        return pltpu.make_async_remote_copy(
            src_ref=src, dst_ref=dst, send_sem=send, recv_sem=recv, device_id=device, device_id_type=MESH
        )

    def greet(axis, index, size):
        def signal(d):
            other = lax.rem(index + d, size)
            pl.semaphore_signal(barrier, inc=1, device_id={axis: other}, device_id_type=MESH)

        each(1, size, signal)

    greet("chan", column, groups_chan)
    greet("seq", place, parts)

    param_copies = [
        pltpu.make_async_copy(ref, params.at[i], param_sem.at[i]) for i, ref in enumerate((res_h, logr_h))
    ]
    for copy in param_copies:
        copy.start()

    def fetch(i, ref, block):
        return pltpu.make_async_copy(ref.at[:, block_lanes(block)], ins.at[i, block], in_sem.at[i, block])

    whole_inputs = (sig_h, gate_h, outer_h, cot_h)

    def turn(i):
        return lax.rem(own * per + per + i, local)

    @pl.loop(0, local)
    def _(i):
        for rep in range(reps):
            for n, ref in enumerate(whole_inputs):
                fetch(n, ref, rep * local + turn(i)).start()

    for copy in param_copies:
        copy.wait()
    res, logr = params.at[0], params.at[1]

    def piece_copy(sender, fb, d, device):
        ref = edges.at[sender, fb]
        return remote(ref, ref, edge_send.at[d, fb], edge_recv.at[d, fb], device)

    def edge_copy(sender, receiver, fb, d, device):
        first = jnp.where(receiver > sender, 0, reps)
        ref = edges.at[sender, fb, pl.ds(first, reps)]
        return remote(ref, ref, edge_send.at[d, fb], edge_recv.at[d, fb], device)

    @pl.loop(0, local)
    def _(i):
        fb = turn(i)
        for rep in range(reps):
            for n, ref in enumerate(whole_inputs):
                fetch(n, ref, rep * local + fb).wait()
        state_block(
            scale, place, fb, local, filter_lanes(fb, cols, filters), ins, res, logr, g_s, w_s, gt, wt, h_s, pw_s, st,
            lag_s, xs, ys, edges,
        )

        @pl.when(i == 0)
        def _():
            pl.semaphore_wait(barrier, parts - 1 + groups_chan - 1)

        def send(d):
            other = lax.rem(place + d, parts)
            whose = lax.rem(other, owners)
            is_piece = jnp.logical_and(fb >= whose * per, fb < (whose + 1) * per)

            @pl.when(is_piece)
            def _():
                piece_copy(place, fb, d, {"seq": other}).start()

            @pl.when(jnp.logical_not(is_piece))
            def _():
                edge_copy(place, other, fb, d, {"seq": other}).start()

        each(1, parts, send)

    def inner(first, last):
        if first == last:
            return

        @pl.loop(first, last)
        def _(block):
            fb = lax.rem(block, local)
            inner_block(rows, g_s.at[block], w_s.at[block], h_s.at[fb], conv.at[block], grad.at[block])

    half = blocks // 2
    inner(0, half)

    def piece_arrived(d):
        source = lax.rem(place + parts - d, parts)
        for i in range(per):
            piece_copy(source, own * per + i, d, {"seq": source}).wait_recv()

    each(1, parts, piece_arrived)
    for i in range(per):
        fb = own * per + i
        first, second = gradient_block(scale, rows, fb, filter_lanes(fb, cols, filters), edges, res, logr)
        slots[column, i, 0] = first.astype(bf16)
        slots[column, i, 1] = second.astype(bf16)

    def middle(d, back=False):
        other = lax.rem(column + (groups_chan - d if back else d), groups_chan)
        slot = slots.at[other if back else column]
        return remote(slot, slot, mid_send.at[d], mid_recv.at[d], {"chan": other})

    def ending(d, back=False):
        other = lax.rem(own + (owners - d if back else d), owners)
        slot = final.at[other if back else own]
        return remote(slot, slot, end_send.at[d], end_recv.at[d], {"seq": cell + other})

    each(1, groups_chan, lambda d: middle(d).start())
    inner(half, blocks)

    def edge_arrived(d):
        source = lax.rem(place + parts - d, parts)
        for i in range(local - per):
            edge_copy(source, place, turn(i), d, {"seq": source}).wait_recv()

    each(1, parts, edge_arrived)

    def outputs(first, last):
        if first == last:
            return

        @pl.loop(first, last)
        def _(block):
            fb = lax.rem(block, local)
            rep = block // local
            fl = filter_lanes(fb, cols, filters)
            carry_block(rows, fb, rep, fl, edges, logr, carry)
            output_block(
                scale, fl, res, logr, conv.at[block], grad.at[block], xs.at[block], ys.at[block], carry, a_s, p_s, q_s
            )
            d = grad[block]
            at = block_lanes(block)
            out_sig[:, at] = (d * ins[1, block].astype(f32)).astype(bf16)
            out_gate[:, at] = (d * ins[0, block].astype(f32)).astype(bf16)
            out_outer[:, at] = (conv[block] * ins[3, block].astype(f32)).astype(bf16)

    stop = blocks * 5 // 8
    outputs(0, stop)
    each(1, groups_chan, lambda d: middle(d, back=True).wait_recv())
    for kind in range(kinds):
        total = slots[kind].astype(f32)
        for source in range(kind + kinds, groups_chan, kinds):
            total = total + slots[source].astype(f32)
        final[own, kind] = norm * total
    each(1, owners, lambda d: ending(d).start())
    outputs(stop, blocks)
    each(1, owners, lambda d: ending(d, back=True).wait_recv())
    for owner in range(owners):
        for kind in range(kinds):
            for i in range(per):
                first = (kind * local + owner * per + i) * LANES
                for which in range(2):
                    sums[which, :, first : first + LANES] = final[owner, kind, i, which]

    def edge_sent(d):
        other = lax.rem(place + d, parts)
        whose = lax.rem(other, owners)
        for i in range(local):
            fb = lax.rem(whose * per + i, local)
            if i < per:
                piece_copy(place, fb, d, {"seq": other}).wait_send()
            else:
                edge_copy(place, other, fb, d, {"seq": other}).wait_send()

    each(1, parts, edge_sent)
    each(1, groups_chan, lambda d: middle(d).wait_send())
    each(1, owners, lambda d: ending(d).wait_send())


def pass_kernel(sig, gate, outer, sums, out_sig, out_gate, out_outer, out_res, out_rate, sem):
    pairs = ((sig, out_sig), (gate, out_gate), (outer, out_outer), (sums.at[0], out_res), (sums.at[1], out_rate))
    copies = [pltpu.make_async_copy(src, dst, sem.at[n]) for n, (src, dst) in enumerate(pairs)]
    for copy in copies:
        copy.start()
    for copy in copies:
        copy.wait()


def on_device(signal_in, gate_in, outer_gate, cotangent, residues, log_rates):
    parts = lax.axis_size("seq")
    groups_chan = lax.axis_size("chan")
    rows, cols = signal_in.shape
    modes, filters = residues.shape
    total = parts * rows
    blocks = cols // LANES
    segs = rows // SEG
    local = min(cols, filters) // LANES
    owners = math.gcd(parts, local)
    per = local // owners
    kinds = filters // LANES // local
    reps = blocks // local
    scale = float(total) ** (-0.5)
    norm = float(total * cols * groups_chan // filters) ** (-0.5)
    whole = pl.BlockSpec(memory_space=pltpu.VMEM)
    far = pl.BlockSpec(memory_space=pl.ANY)
    shape = jax.ShapeDtypeStruct
    tiles = pltpu.VMEM((blocks, rows, LANES), f32)
    states = pltpu.VMEM((blocks, segs * modes, LANES), f32)
    phases = pltpu.VMEM((reps, segs // PACK, SEG * PACK, LANES), bf16)
    dma = pltpu.SemaphoreType.DMA
    narrow = shape((rows, cols), bf16)
    near = pltpu.VMEM((rows, cols), bf16)
    results = pl.pallas_call(
        functools.partial(whole_kernel, scale, norm, parts, groups_chan, owners),
        out_shape=(near, near, near, pltpu.VMEM((2, modes, filters), f32)),
        in_specs=[pl.BlockSpec(memory_space=pltpu.HBM)] * 6,
        out_specs=(whole,) * 4,
        scratch_shapes=[
            pltpu.VMEM((4, blocks, rows, LANES), bf16),
            pltpu.VMEM((2, modes, filters), f32),
            tiles,
            tiles,
            tiles,
            tiles,
            states,
            states,
            pltpu.VMEM((parts, local, 4 * reps + 2, modes, LANES), bf16),
            pltpu.VMEM((2, modes, LANES), f32),
            pltpu.VMEM((local, SEG, LANES), f32),
            phases,
            phases,
            pltpu.VMEM((modes, LANES), f32),
            pltpu.VMEM(((SEG + 1) * modes, LANES), f32),
            pltpu.VMEM((reps, 4, modes * segs, LANES), f32),
            pltpu.VMEM((SEG * SUB, LANES), f32),
            pltpu.VMEM((segs * modes, LANES), f32),
            pltpu.VMEM((segs * modes, LANES), f32),
            pltpu.VMEM((groups_chan, per, 2, modes, LANES), bf16),
            pltpu.VMEM((owners, kinds, per, 2, modes, LANES), f32),
            dma((4, blocks)),
            dma((2,)),
            dma((parts, local)),
            dma((parts, local)),
            dma((groups_chan,)),
            dma((groups_chan,)),
            dma((owners,)),
            dma((owners,)),
        ],
        compiler_params=pltpu.CompilerParams(
            collective_id=0, has_side_effects=True
        ),
        name="whole",
    )(signal_in, gate_in, outer_gate, cotangent, residues, log_rates)
    results = [pltpu.with_memory_space_constraint(a, pltpu.VMEM) for a in results]
    return pl.pallas_call(
        pass_kernel,
        out_shape=(narrow, narrow, narrow, shape((modes, filters), f32), shape((modes, filters), f32)),
        in_specs=[whole] * 4,
        out_specs=(far,) * 5,
        scratch_shapes=[dma((5,))],
        name="passed",
    )(*results)


def solution(mesh):
    placed = (P("seq", "chan"), P("seq", "chan"), P("seq", "chan"), P("seq", "chan"), P(), P())
    return jax.shard_map(
        on_device,
        mesh=mesh,
        in_specs=placed,
        out_specs=(P("seq", "chan"), P("seq", "chan"), P("seq", "chan"), P(), P()),
        check_vma=False,
    )
```

time: 30.4 us -> 21.6 us (0.71)
  Pallas kernels: 29.6 us -> 20.7 us
    pallas_call x1, Pallas kernels: 28.4 us -> 19.6 us  [on_device(): pl.pallas_call(functools.partial(whole_kernel, scale, norm, parts, groups...]
where the time goes in v2:
time: 21.6 us; the launch traced here: 21.4 us
  Pallas kernels  20.7 us (96%)
  between operations  0.64 us (3%)
    pallas_call x1, Pallas kernels, on_device(): pl.pallas_call(functools.partial(whole_kernel, scale, norm, parts, groups...  19.6 us
    pallas_call x1, Pallas kernels, on_device(): pl.pallas_call(pass_kernel, out_shape=(narrow, narrow, narrow, shape((mod...  1.19 us

profile of v2, /device:TPU:0, one launch (start us, length us, event | category | flops | bytes accessed | tf_op | source)
XLA Modules:
  0.0 21.4 jit_solution(10611261969900327476)
XLA Ops:
  0.6 19.6 %whole.1 = (bf16[256,1024]{1,0:T(8,128)(2,1)S(1)}, bf16[256,1024]{1,0:T(8,128)(2,1)S(1)}, bf16[256,1024]{1,0:T(8,128)(2,1)S(1)}, f32[2,16,512]{2,1,0:T(8,128)S(1)}) custom-call(bf16[256,1024]{1,0:T(8,128)(2,1)} %sig_h.1, bf16[256,1024]{1,0:T(8,128)(2,1)} %gate_h.1, bf16[256,1024]{1,0:T(8,128)(2,1)} %outer_h.1, bf16[256,1024]{1,0:T(8,128)(2,1)} %cot_h.1, ...), custom_call_target="tpu_custom_call" | custom-call | tf_op jit(solution)/shard_map/whole/pallas_call | solution.py:483
  20.2 1.2 %passed.1 = (bf16[256,1024]{1,0:T(8,128)(2,1)}, bf16[256,1024]{1,0:T(8,128)(2,1)}, bf16[256,1024]{1,0:T(8,128)(2,1)}, f32[16,512]{1,0:T(8,128)}, f32[16,512]{1,0:T(8,128)}) custom-call(bf16[256,1024]{1,0:T(8,128)(2,1)S(1)} %get-tuple-element.9.sig, bf16[256,1024]{1,0:T(8,128)(2,1)S(1)} %get-tuple-element.10.gate, ...), custom_call_target="tpu_custom_call" | custom-call | tf_op jit(solution)/shard_map/passed/pallas_call | solution.py:525

commit v3 on v2

--- a/solution.py
+++ b/solution.py
@@ -12,6 +12,7 @@
 SUB = 8
 SEG = 16
 PACK = 16
+PITCH = SEG + 1
 f32 = jnp.float32
 bf16 = jnp.bfloat16
 MESH = pl.DeviceIdType.MESH
@@ -51,7 +52,7 @@
         p = [terms[first]]
         for term in terms[first + 1 : first + 4]:
             p.append(p[-1] + term)
-        quads.append(p[3])
+        quads.append(p[-1])
         weighted.append(tree(p if last else p[:3]))
     q = [quads[0]]
     for quad in quads[1:]:
@@ -59,10 +60,11 @@
     return q[-1], tree(weighted) + 4.0 * tree(q[:-1])
 
 
-def state_block(scale, place, fb, local, fl, ins, res, logr, g_s, w_s, gt, wt, h_s, pw_s, st, lag_s, xs, ys, edges):
-    rows = g_s.shape[1]
+def state_block(scale, place, fb, local, fl, ins, res, logr, g_s, w_s, gt, wt, h_s, pw_s, less_s, plain, st, lag_s, xs, ys,
+                edges):
     modes = res.shape[0]
-    segs = rows // SEG
+    segs = g_s.shape[1] // PITCH
+    hop = segs + 1
     reps = g_s.shape[0] // local
     rate = jnp.exp(logr[:, fl])
     amp = res[:, fl] * scale
@@ -70,6 +72,7 @@
     power = jnp.ones((modes, LANES), f32)
     for u in range(SEG + 1):
         pw_s[u * modes : (u + 1) * modes, :] = power
+        less_s[u * modes : (u + 1) * modes, :] = power - 1.0
         if u < SEG:
             h_s[fb, u : u + 1, :] = jnp.sum(amp * power, 0, keepdims=True)
             power = power * a
@@ -78,28 +81,40 @@
     for rep in range(reps):
         block = rep * local + fb
         sig, gate, outer, cot = (ins[i, block].astype(f32) for i in range(4))
-        g_s[block] = (sig * gate).astype(bf16).astype(f32)
-        w_s[block] = (cot * outer).astype(bf16).astype(f32)
-        for src, dst in ((g_s.at[block], gt), (w_s.at[block], wt)):
+        g = (sig * gate).astype(bf16).astype(f32)
+        w = (cot * outer).astype(bf16).astype(f32)
+        for seg in range(segs):
+            g_s[block, seg * PITCH : seg * PITCH + SEG, :] = g[seg * SEG : (seg + 1) * SEG]
+            w_s[block, seg * PITCH : seg * PITCH + SEG, :] = w[seg * SEG : (seg + 1) * SEG]
+        for i, (src, dst) in enumerate(((g_s.at[block], gt), (w_s.at[block], wt))):
             for part in range(segs // PACK):
-                base = part * PACK * SEG
-                for j in range(SEG):
-                    halves = [rows_of(src, base + half * SUB * SEG + j, SEG) for half in range(PACK // SUB)]
-                    dst[rep, part, j * PACK : (j + 1) * PACK, :] = jnp.concatenate(halves, 0).astype(bf16)
+                base = part * PACK * PITCH
+                running = jnp.zeros((PACK, LANES), f32)
+                weighted = running
+                for j in range(SEG) if i == 0 else reversed(range(SEG)):
+                    halves = [rows_of(src, base + half * SUB * PITCH + j, PITCH) for half in range(PACK // SUB)]
+                    value = jnp.concatenate(halves, 0)
+                    dst[rep, part, j * PACK : (j + 1) * PACK, :] = value.astype(bf16)
+                    running = running + value
+                    if i == 0 or j > 0:
+                        weighted = weighted + running
+                at = slice(part * PACK, (part + 1) * PACK)
+                plain[rep, 2 * i, at, :] = running
+                plain[rep, 2 * i + 1, at, :] = weighted
 
     def phase(ref, rep, part, j):
         return ref[rep, part, j * PACK : (j + 1) * PACK, :]
 
     for k in range(modes):
-        powers = [spread_narrow(pw_s, e * modes + k) for e in range(SEG + 1)]
+        powers = [spread_narrow(less_s, e * modes + k) for e in range(1, SEG + 1)]
         for rep in range(reps):
             for part in range(segs // PACK):
-                x, d = moments([powers[SEG - j] * phase(gt, rep, part, j) for j in range(SEG)], True)
-                back = [powers[j] * phase(wt, rep, part, j) for j in range(SEG - 1, 0, -1)]
-                y, v = moments(back + [phase(wt, rep, part, 0)], False)
-                at = slice(k * segs + part * PACK, k * segs + (part + 1) * PACK)
+                x, d = moments([powers[SEG - 1 - j] * phase(gt, rep, part, j) for j in range(SEG)], True)
+                y, v = moments([powers[j - 1] * phase(wt, rep, part, j) for j in range(SEG - 1, 0, -1)], False)
+                rows = slice(part * PACK, (part + 1) * PACK)
+                at = slice(k * hop + part * PACK, k * hop + (part + 1) * PACK)
                 for i, value in enumerate((x, d, y, v)):
-                    st[rep, i, at, :] = value.astype(f32)
+                    st[rep, i, at, :] = plain[rep, i, rows, :] + value.astype(f32)
 
     lags = [None] * SEG
     for rep in range(reps):
@@ -127,7 +142,7 @@
         block = rep * local + fb
         x, xd = zero, zero
         for seg in range(segs):
-            at = pl.ds(seg, modes, stride=segs)
+            at = pl.ds(seg, modes, stride=hop)
             e, d, y, v = (st[rep, i, at, :] for i in range(4))
             xs[block, seg * modes : (seg + 1) * modes, :] = x
             if seg > 0:
@@ -137,7 +152,7 @@
             x = seg_decay * x + e
         y, yv = zero, zero
         for seg in reversed(range(segs)):
-            at = pl.ds(seg, modes, stride=segs)
+            at = pl.ds(seg, modes, stride=hop)
             ys[block, seg * modes : (seg + 1) * modes, :] = y
             yv = st[rep, 3, at, :] + seg_decay * (yv + float(SEG) * y)
             y = st[rep, 2, at, :] + seg_decay * y
@@ -147,23 +162,23 @@
     edges[place, fb, 4 * reps + 1] = gl.astype(bf16)
 
 
-def inner_block(rows, g_s, w_s, h_s, conv, grad):
-    @pl.loop(0, rows // (SEG * SUB))
+def inner_block(g_s, w_s, h_s, conv, grad):
+    @pl.loop(0, g_s.shape[0] // (PITCH * SUB))
     def _(group):
-        base = group * (SUB * SEG)
+        base = group * (SUB * PITCH)
         h = [spread(h_s, u) for u in range(SEG)]
-        g = [rows_of(g_s, base + j, SEG) for j in range(SEG)]
+        g = [rows_of(g_s, base + j, PITCH) for j in range(SEG)]
         for j in range(SEG):
             forward = h[0] * g[j]
             for u in range(1, j + 1):
                 forward = forward + h[u] * g[j - u]
-            conv[pl.ds(base + j, SUB, stride=SEG), :] = forward
-        w = [rows_of(w_s, base + j, SEG) for j in range(SEG)]
+            conv[pl.ds(base + j, SUB, stride=PITCH), :] = forward
+        w = [rows_of(w_s, base + j, PITCH) for j in range(SEG)]
         for j in range(SEG):
             backward = h[0] * w[j]
             for u in range(1, SEG - j):
                 backward = backward + h[u] * w[j + u]
-            grad[pl.ds(base + j, SUB, stride=SEG), :] = backward
+            grad[pl.ds(base + j, SUB, stride=PITCH), :] = backward
 
 
 def gradient_block(scale, span, fb, fl, edges, res, logr):
@@ -210,9 +225,9 @@
 
 
 def output_block(scale, fl, res, logr, conv, grad, xs, ys, carry, a_s, p_s, q_s):
-    rows = conv.shape[0]
     modes = res.shape[0]
-    segs = rows // SEG
+    segs = conv.shape[0] // PITCH
+    hop = modes + 1
     rate = jnp.exp(logr[:, fl])
     amp = res[:, fl] * scale
     a_s[...] = jnp.exp(-rate)
@@ -220,26 +235,24 @@
     p = amp * carry[0]
     q = amp * carry[1]
     for seg in range(segs):
-        at = slice(seg * modes, (seg + 1) * modes)
-        p_s[at, :] = amp * xs[at, :] + p
+        p_s[seg * hop : seg * hop + modes, :] = amp * xs[seg * modes : (seg + 1) * modes, :] + p
         p = p * seg_decay
         back = segs - 1 - seg
-        at = slice(back * modes, (back + 1) * modes)
-        q_s[at, :] = amp * ys[at, :] + q
+        q_s[back * hop : back * hop + modes, :] = amp * ys[back * modes : (back + 1) * modes, :] + q
         q = q * seg_decay
 
     @pl.loop(0, segs // SUB)
     def _(group):
-        base = group * (SUB * SEG)
+        base = group * (SUB * PITCH)
         for half in range(0, modes, SUB):
             decay = [spread(a_s, half + k) for k in range(SUB)]
-            p = [rows_of(p_s, group * (SUB * modes) + half + k, modes) for k in range(SUB)]
-            q = [rows_of(q_s, group * (SUB * modes) + half + k, modes) for k in range(SUB)]
+            p = [rows_of(p_s, group * (SUB * hop) + half + k, hop) for k in range(SUB)]
+            q = [rows_of(q_s, group * (SUB * hop) + half + k, hop) for k in range(SUB)]
             for j in range(SEG):
-                at = pl.ds(base + j, SUB, stride=SEG)
+                at = pl.ds(base + j, SUB, stride=PITCH)
                 conv[at, :] = conv[at, :] + tree(p)
                 q = [decay[k] * q[k] for k in range(SUB)]
-                at = pl.ds(base + SEG - 1 - j, SUB, stride=SEG)
+                at = pl.ds(base + SEG - 1 - j, SUB, stride=PITCH)
                 grad[at, :] = grad[at, :] + tree(q)
                 if j < SEG - 1:
                     p = [decay[k] * p[k] for k in range(SUB)]
@@ -250,7 +263,7 @@
     sig_h, gate_h, outer_h, cot_h, res_h, logr_h,
     out_sig, out_gate, out_outer, sums,
     ins, params, g_s, w_s, conv, grad, xs, ys, edges, carry, h_s, gt, wt,
-    a_s, pw_s, st, lag_s, p_s, q_s, slots, final,
+    a_s, pw_s, less_s, plain, st, lag_s, p_s, q_s, slots, final,
     in_sem, param_sem, edge_send, edge_recv, mid_send, mid_recv, end_send, end_recv,
 ):
     rows, cols = sig_h.shape
@@ -328,8 +341,8 @@
             for n, ref in enumerate(whole_inputs):
                 fetch(n, ref, rep * local + fb).wait()
         state_block(
-            scale, place, fb, local, filter_lanes(fb, cols, filters), ins, res, logr, g_s, w_s, gt, wt, h_s, pw_s, st,
-            lag_s, xs, ys, edges,
+            scale, place, fb, local, filter_lanes(fb, cols, filters), ins, res, logr, g_s, w_s, gt, wt, h_s, pw_s,
+            less_s, plain, st, lag_s, xs, ys, edges,
         )
 
         @pl.when(i == 0)
@@ -358,7 +371,7 @@
         @pl.loop(first, last)
         def _(block):
             fb = lax.rem(block, local)
-            inner_block(rows, g_s.at[block], w_s.at[block], h_s.at[fb], conv.at[block], grad.at[block])
+            inner_block(g_s.at[block], w_s.at[block], h_s.at[fb], conv.at[block], grad.at[block])
 
     half = blocks // 2
     inner(0, half)
@@ -408,11 +421,14 @@
             output_block(
                 scale, fl, res, logr, conv.at[block], grad.at[block], xs.at[block], ys.at[block], carry, a_s, p_s, q_s
             )
-            d = grad[block]
             at = block_lanes(block)
-            out_sig[:, at] = (d * ins[1, block].astype(f32)).astype(bf16)
-            out_gate[:, at] = (d * ins[0, block].astype(f32)).astype(bf16)
-            out_outer[:, at] = (conv[block] * ins[3, block].astype(f32)).astype(bf16)
+            for seg in range(rows // SEG):
+                own_rows = slice(seg * SEG, (seg + 1) * SEG)
+                d = grad[block, seg * PITCH : seg * PITCH + SEG, :]
+                c = conv[block, seg * PITCH : seg * PITCH + SEG, :]
+                out_sig[own_rows, at] = (d * ins[1, block, own_rows, :].astype(f32)).astype(bf16)
+                out_gate[own_rows, at] = (d * ins[0, block, own_rows, :].astype(f32)).astype(bf16)
+                out_outer[own_rows, at] = (c * ins[3, block, own_rows, :].astype(f32)).astype(bf16)
 
     stop = blocks * 5 // 8
     outputs(0, stop)
@@ -474,7 +490,7 @@
     whole = pl.BlockSpec(memory_space=pltpu.VMEM)
     far = pl.BlockSpec(memory_space=pl.ANY)
     shape = jax.ShapeDtypeStruct
-    tiles = pltpu.VMEM((blocks, rows, LANES), f32)
+    tiles = pltpu.VMEM((blocks, segs * PITCH, LANES), f32)
     states = pltpu.VMEM((blocks, segs * modes, LANES), f32)
     phases = pltpu.VMEM((reps, segs // PACK, SEG * PACK, LANES), bf16)
     dma = pltpu.SemaphoreType.DMA
@@ -501,10 +517,12 @@
             phases,
             pltpu.VMEM((modes, LANES), f32),
             pltpu.VMEM(((SEG + 1) * modes, LANES), f32),
-            pltpu.VMEM((reps, 4, modes * segs, LANES), f32),
+            pltpu.VMEM(((SEG + 1) * modes, LANES), f32),
+            pltpu.VMEM((reps, 4, segs, LANES), f32),
+            pltpu.VMEM((reps, 4, modes * (segs + 1), LANES), f32),
             pltpu.VMEM((SEG * SUB, LANES), f32),
-            pltpu.VMEM((segs * modes, LANES), f32),
-            pltpu.VMEM((segs * modes, LANES), f32),
+            pltpu.VMEM((segs * (modes + 1), LANES), f32),
+            pltpu.VMEM((segs * (modes + 1), LANES), f32),
             pltpu.VMEM((groups_chan, per, 2, modes, LANES), bf16),
             pltpu.VMEM((owners, kinds, per, 2, modes, LANES), f32),
             dma((4, blocks)),

time: 21.6 us -> 20.1 us (0.931)
  Pallas kernels: 20.7 us -> 19.3 us
    pallas_call x1, Pallas kernels: 19.6 us -> 18.1 us  [on_device(): pl.pallas_call(functools.partial(whole_kernel, scale, norm, parts, groups...]
where the time goes in v3:
time: 20.1 us; the launch traced here: 20 us
  Pallas kernels  19.3 us (96%)
  between operations  0.64 us (3%)
    pallas_call x1, Pallas kernels, on_device(): pl.pallas_call(functools.partial(whole_kernel, scale, norm, parts, groups...  18.1 us
    pallas_call x1, Pallas kernels, on_device(): pl.pallas_call(pass_kernel, out_shape=(narrow, narrow, narrow, shape((mod...  1.19 us

profile of v3, /device:TPU:0, one launch (start us, length us, event | category | flops | bytes accessed | tf_op | source)
XLA Modules:
  0.0 20.0 jit_solution(13007751213468302425)
XLA Ops:
  0.6 18.1 %whole.1 = (bf16[256,1024]{1,0:T(8,128)(2,1)S(1)}, bf16[256,1024]{1,0:T(8,128)(2,1)S(1)}, bf16[256,1024]{1,0:T(8,128)(2,1)S(1)}, f32[2,16,512]{2,1,0:T(8,128)S(1)}) custom-call(bf16[256,1024]{1,0:T(8,128)(2,1)} %sig_h.1, bf16[256,1024]{1,0:T(8,128)(2,1)} %gate_h.1, bf16[256,1024]{1,0:T(8,128)(2,1)} %outer_h.1, bf16[256,1024]{1,0:T(8,128)(2,1)} %cot_h.1, ...), custom_call_target="tpu_custom_call" | custom-call | tf_op jit(solution)/shard_map/whole/pallas_call | solution.py:499
  18.8 1.2 %passed.1 = (bf16[256,1024]{1,0:T(8,128)(2,1)}, bf16[256,1024]{1,0:T(8,128)(2,1)}, bf16[256,1024]{1,0:T(8,128)(2,1)}, f32[16,512]{1,0:T(8,128)}, f32[16,512]{1,0:T(8,128)}) custom-call(bf16[256,1024]{1,0:T(8,128)(2,1)S(1)} %get-tuple-element.9.sig, bf16[256,1024]{1,0:T(8,128)(2,1)S(1)} %get-tuple-element.10.gate, ...), custom_call_target="tpu_custom_call" | custom-call | tf_op jit(solution)/shard_map/passed/pallas_call | solution.py:543

commit v4 on v3

--- a/solution.py
+++ b/solution.py
@@ -80,9 +80,8 @@
 
     for rep in range(reps):
         block = rep * local + fb
-        sig, gate, outer, cot = (ins[i, block].astype(f32) for i in range(4))
-        g = (sig * gate).astype(bf16).astype(f32)
-        w = (cot * outer).astype(bf16).astype(f32)
+        g = (ins[0, block] * ins[1, block]).astype(f32)
+        w = (ins[3, block] * ins[2, block]).astype(f32)
         for seg in range(segs):
             g_s[block, seg * PITCH : seg * PITCH + SEG, :] = g[seg * SEG : (seg + 1) * SEG]
             w_s[block, seg * PITCH : seg * PITCH + SEG, :] = w[seg * SEG : (seg + 1) * SEG]
@@ -156,10 +155,10 @@
             ys[block, seg * modes : (seg + 1) * modes, :] = y
             yv = st[rep, 3, at, :] + seg_decay * (yv + float(SEG) * y)
             y = st[rep, 2, at, :] + seg_decay * y
-        for i, value in enumerate((x, y, xd, yv)):
-            edges[place, fb, i * reps + rep] = value.astype(bf16)
-    edges[place, fb, 4 * reps] = gr.astype(bf16)
-    edges[place, fb, 4 * reps + 1] = gl.astype(bf16)
+        for first, value in ((0, x), (reps, xd), (2 * reps + 2, y), (3 * reps + 2, yv)):
+            edges[place, fb, first + rep] = value.astype(bf16)
+    edges[place, fb, 2 * reps] = gr.astype(bf16)
+    edges[place, fb, 2 * reps + 1] = gl.astype(bf16)
 
 
 def inner_block(g_s, w_s, h_s, conv, grad):
@@ -190,17 +189,17 @@
     def value(source, i):
         return edges[source, fb, i].astype(f32)
 
-    gr = tree([value(source, 4 * reps) for source in range(parts)])
-    gl = tree([value(source, 4 * reps + 1) for source in range(parts)])
+    gr = tree([value(source, 2 * reps) for source in range(parts)])
+    gl = tree([value(source, 2 * reps + 1) for source in range(parts)])
     for rep in range(reps):
         x = value(0, rep)
-        xd = value(0, 2 * reps + rep)
+        xd = value(0, reps + rep)
         for source in range(1, parts):
-            y = value(source, reps + rep)
+            y = value(source, 2 * reps + 2 + rep)
             gr = gr + x * y
-            gl = gl + (x * value(source, 3 * reps + rep) + xd * y)
+            gl = gl + (x * value(source, 3 * reps + 2 + rep) + xd * y)
             if source < parts - 1:
-                xd = (xd + float(span) * x) * decay + value(source, 2 * reps + rep)
+                xd = (xd + float(span) * x) * decay + value(source, reps + rep)
                 x = x * decay + value(source, rep)
     return scale * gr, -scale * (res[:, fl] * rate) * gl
 
@@ -212,7 +211,7 @@
     decay = jnp.exp(-jnp.exp(logr[:, fl]) * float(span))
     values = []
     for source in range(parts):
-        which = jnp.where(source > place, reps, 0)
+        which = jnp.where(source > place, 2 * reps + 2, 0)
         values.append(edges[source, fb, which + rep].astype(f32))
     x = jnp.zeros(decay.shape, f32)
     y = x
@@ -298,9 +297,6 @@
 
         each(1, size, signal)
 
-    greet("chan", column, groups_chan)
-    greet("seq", place, parts)
-
     param_copies = [
         pltpu.make_async_copy(ref, params.at[i], param_sem.at[i]) for i, ref in enumerate((res_h, logr_h))
     ]
@@ -321,16 +317,28 @@
             for n, ref in enumerate(whole_inputs):
                 fetch(n, ref, rep * local + turn(i)).start()
 
+    greet("chan", column, groups_chan)
+    greet("seq", place, parts)
+
     for copy in param_copies:
         copy.wait()
     res, logr = params.at[0], params.at[1]
 
-    def piece_copy(sender, fb, d, device):
-        ref = edges.at[sender, fb]
-        return remote(ref, ref, edge_send.at[d, fb], edge_recv.at[d, fb], device)
+    def piece_copy(sender, fb, d, device, act):
+        at_end = jnp.logical_or(sender == 0, sender == parts - 1)
+
+        @pl.when(at_end)
+        def _():
+            ref = edges.at[sender, fb, pl.ds(jnp.where(sender == 0, 0, 2 * reps), 2 * reps + 2)]
+            act(remote(ref, ref, edge_send.at[d, fb], edge_recv.at[d, fb], device))
+
+        @pl.when(jnp.logical_not(at_end))
+        def _():
+            ref = edges.at[sender, fb]
+            act(remote(ref, ref, edge_send.at[d, fb], edge_recv.at[d, fb], device))
 
     def edge_copy(sender, receiver, fb, d, device):
-        first = jnp.where(receiver > sender, 0, reps)
+        first = jnp.where(receiver > sender, 0, 2 * reps + 2)
         ref = edges.at[sender, fb, pl.ds(first, reps)]
         return remote(ref, ref, edge_send.at[d, fb], edge_recv.at[d, fb], device)
 
@@ -356,7 +364,7 @@
 
             @pl.when(is_piece)
             def _():
-                piece_copy(place, fb, d, {"seq": other}).start()
+                piece_copy(place, fb, d, {"seq": other}, lambda copy: copy.start())
 
             @pl.when(jnp.logical_not(is_piece))
             def _():
@@ -373,13 +381,13 @@
             fb = lax.rem(block, local)
             inner_block(g_s.at[block], w_s.at[block], h_s.at[fb], conv.at[block], grad.at[block])
 
-    half = blocks // 2
+    half = blocks // 4
     inner(0, half)
 
     def piece_arrived(d):
         source = lax.rem(place + parts - d, parts)
         for i in range(per):
-            piece_copy(source, own * per + i, d, {"seq": source}).wait_recv()
+            piece_copy(source, own * per + i, d, {"seq": source}, lambda copy: copy.wait_recv())
 
     each(1, parts, piece_arrived)
     for i in range(per):
@@ -430,36 +438,36 @@
                 out_gate[own_rows, at] = (d * ins[0, block, own_rows, :].astype(f32)).astype(bf16)
                 out_outer[own_rows, at] = (c * ins[3, block, own_rows, :].astype(f32)).astype(bf16)
 
-    stop = blocks * 5 // 8
+    stop = blocks // 2
     outputs(0, stop)
     each(1, groups_chan, lambda d: middle(d, back=True).wait_recv())
     for kind in range(kinds):
         total = slots[kind].astype(f32)
         for source in range(kind + kinds, groups_chan, kinds):
             total = total + slots[source].astype(f32)
-        final[own, kind] = norm * total
+        final[own, kind] = (norm * total).astype(bf16)
     each(1, owners, lambda d: ending(d).start())
     outputs(stop, blocks)
+    def edge_sent(d):
+        other = lax.rem(place + d, parts)
+        whose = lax.rem(other, owners)
+        for i in range(local):
+            fb = lax.rem(whose * per + i, local)
+            if i < per:
+                piece_copy(place, fb, d, {"seq": other}, lambda copy: copy.wait_send())
+            else:
+                edge_copy(place, other, fb, d, {"seq": other}).wait_send()
+
+    each(1, parts, edge_sent)
+    each(1, groups_chan, lambda d: middle(d).wait_send())
     each(1, owners, lambda d: ending(d, back=True).wait_recv())
     for owner in range(owners):
         for kind in range(kinds):
             for i in range(per):
                 first = (kind * local + owner * per + i) * LANES
                 for which in range(2):
-                    sums[which, :, first : first + LANES] = final[owner, kind, i, which]
-
-    def edge_sent(d):
-        other = lax.rem(place + d, parts)
-        whose = lax.rem(other, owners)
-        for i in range(local):
-            fb = lax.rem(whose * per + i, local)
-            if i < per:
-                piece_copy(place, fb, d, {"seq": other}).wait_send()
-            else:
-                edge_copy(place, other, fb, d, {"seq": other}).wait_send()
-
-    each(1, parts, edge_sent)
-    each(1, groups_chan, lambda d: middle(d).wait_send())
+                    sums[which, :, first : first + LANES] = final[owner, kind, i, which].astype(f32)
+
     each(1, owners, lambda d: ending(d).wait_send())
 
 
@@ -524,7 +532,7 @@
             pltpu.VMEM((segs * (modes + 1), LANES), f32),
             pltpu.VMEM((segs * (modes + 1), LANES), f32),
             pltpu.VMEM((groups_chan, per, 2, modes, LANES), bf16),
-            pltpu.VMEM((owners, kinds, per, 2, modes, LANES), f32),
+            pltpu.VMEM((owners, kinds, per, 2, modes, LANES), bf16),
             dma((4, blocks)),
             dma((2,)),
             dma((parts, local)),

time: 20.1 us -> 19.5 us (0.970)
  Pallas kernels: 19.3 us -> 18.7 us
    pallas_call x1, Pallas kernels: 18.1 us -> 17.5 us  [on_device(): pl.pallas_call(functools.partial(whole_kernel, scale, norm, parts, groups...]
where the time goes in v4:
time: 19.5 us; the launch traced here: 19.3 us
  Pallas kernels  18.7 us (96%)
  between operations  0.64 us (3%)
    pallas_call x1, Pallas kernels, on_device(): pl.pallas_call(functools.partial(whole_kernel, scale, norm, parts, groups...  17.5 us
    pallas_call x1, Pallas kernels, on_device(): pl.pallas_call(pass_kernel, out_shape=(narrow, narrow, narrow, shape((mod...  1.19 us

profile of v4, /device:TPU:0, one launch (start us, length us, event | category | flops | bytes accessed | tf_op | source)
XLA Modules:
  0.0 19.3 jit_solution(8528088183769369915)
XLA Ops:
  0.6 17.5 %whole.1 = (bf16[256,1024]{1,0:T(8,128)(2,1)S(1)}, bf16[256,1024]{1,0:T(8,128)(2,1)S(1)}, bf16[256,1024]{1,0:T(8,128)(2,1)S(1)}, f32[2,16,512]{2,1,0:T(8,128)S(1)}) custom-call(bf16[256,1024]{1,0:T(8,128)(2,1)} %sig_h.1, bf16[256,1024]{1,0:T(8,128)(2,1)} %gate_h.1, bf16[256,1024]{1,0:T(8,128)(2,1)} %outer_h.1, bf16[256,1024]{1,0:T(8,128)(2,1)} %cot_h.1, ...), custom_call_target="tpu_custom_call" | custom-call | tf_op jit(solution)/shard_map/whole/pallas_call | solution.py:507
  18.1 1.2 %passed.1 = (bf16[256,1024]{1,0:T(8,128)(2,1)}, bf16[256,1024]{1,0:T(8,128)(2,1)}, bf16[256,1024]{1,0:T(8,128)(2,1)}, f32[16,512]{1,0:T(8,128)}, f32[16,512]{1,0:T(8,128)}) custom-call(bf16[256,1024]{1,0:T(8,128)(2,1)S(1)} %get-tuple-element.9.sig, bf16[256,1024]{1,0:T(8,128)(2,1)S(1)} %get-tuple-element.10.gate, ...), custom_call_target="tpu_custom_call" | custom-call | tf_op jit(solution)/shard_map/passed/pallas_call | solution.py:551
